TPU v7x, 128 devices: a whole 4x4x4 slice. The times are simulated.
128 devices in a mesh: row: 8 (over z, y_lo), col: 16 (over x, y_hi, core).
Axes of the slice: x: 4, y: 4 (y_hi: 2, y_lo: 2; y = y_hi * 2 + y_lo), z: 4, core: 2. Of those that a mesh axis runs over, the one named last changes fastest.
Arguments:
- covariance: float32 [16384, 16384], P('row', 'col'), may hold values from -1 to 3, as said below
- center: float32 [16384], replicated, may hold values from 0.4 to 1
- links: float32 [4, 16384], replicated, may hold values from 0.05 to 0.25
- process: float32 [16384], replicated, may hold values from 0.1 to 1
- wells: int32 [1, 256], replicated, may hold values from 0 to 16383, as said below
- noise: float32 [1, 256], replicated, may hold values from 0.05 to 0.5
Outputs:
- updated: float32 [16384, 16384], P('row', 'col')
Inputs may be any that keep to these rules, and one draw needn't show every extreme that they name: `covariance`: symmetric positive definite. `wells`: each row holds 256 distinct cells; at most 32 of them lie in one aligned block of 1024 cells, and exactly 32 in some block.
All inputs are finite; a program needn't handle non-finite values.
Results may differ from a plain program's by a relative error of at most 0.0001.
Values sent between devices are 32-bit elements; how exact they have to be, the bound alone decides.
No kernel may reach another device: no remote copies, remote signals or barrier semaphores. Data moves between devices by JAX's collectives and lax.ppermute only.
A program may use at most 128 MiB of HBM per device.

v0:
```python
import jax
import jax.numpy as jnp
from jax import lax
from jax.sharding import PartitionSpec as P

NGY = 128
M = 256
WMAX = 32


def extended(cells, sides, width):
    for axis, dim in sides:
        count = lax.axis_size(axis)
        ends = count - 1
        head = lax.slice_in_dim(cells, 0, width, axis=dim)
        tail = lax.slice_in_dim(cells, cells.shape[dim] - width, cells.shape[dim], axis=dim)
        cells = jnp.concatenate(
            [
                lax.ppermute(tail, axis, [(i, (i + 1) % count) for i in range(ends)]),
                cells,
                lax.ppermute(head, axis, [((i + 1) % count, i) for i in range(ends)]),
            ],
            axis=dim,
        )
    return cells


def rows_first(arrays, axis, dims):
    turned = [jnp.moveaxis(a, dim, 0) for a, dim in zip(arrays, dims)]
    widths = [t[0].size for t in turned]
    both = jnp.concatenate([t.reshape(-1, w) for t, w in zip(turned, widths)], axis=1)
    result = lax.all_gather(both, axis, axis=0, tiled=True)
    blocks = jnp.split(result, [sum(widths[:k]) for k in range(1, len(widths))], axis=1)
    return tuple(
        (
            jnp.moveaxis(b.reshape(-1, *t.shape[1:]), 0, dim)
            for b, t, dim in zip(blocks, turned, dims)
        )
    )


def shards(covariance, center, links, process, wells, noise):
    row_id = lax.axis_index("row")
    col_id = lax.axis_index("col")
    row_count, col_count = covariance.shape
    grid_rows = row_count // NGY
    grid_cols = col_count // NGY
    row_start = row_id * row_count
    col_start = col_id * col_count
    own_rows = lax.dynamic_slice_in_dim(center, row_start, row_count).reshape(grid_rows, NGY, 1)
    link_rows = lax.dynamic_slice_in_dim(links, row_start, row_count, 1).reshape(
        4, grid_rows, NGY, 1
    )
    own_cols = lax.dynamic_slice_in_dim(center, col_start, col_count).reshape(1, grid_cols, NGY)
    link_cols = lax.dynamic_slice_in_dim(links, col_start, col_count, 1).reshape(
        4, 1, grid_cols, NGY
    )
    noise_rows = lax.dynamic_slice_in_dim(process, row_start, row_count)
    local_rows = jnp.arange(row_count, dtype=jnp.int32)
    diag_cols = row_start + local_rows - col_start
    diag_valid = (diag_cols >= 0) & (diag_cols < col_count)
    diag_clip = jnp.clip(diag_cols, 0, col_count - 1)
    diag_values = jnp.where(diag_valid, noise_rows, 0.0)
    current = covariance
    field = current.reshape(grid_rows, NGY, col_count)
    rimmed = extended(field, (("row", 0),), 1)
    padded = jnp.pad(rimmed, ((0, 0), (1, 1), (0, 0)))
    left = own_rows * field + link_rows[0] * padded[:-2, 1:-1] + link_rows[1] * padded[2:, 1:-1]
    left = left + link_rows[2] * padded[1:-1, :-2] + link_rows[3] * padded[1:-1, 2:]
    field = left.reshape(row_count, grid_cols, NGY)
    rimmed = extended(field, (("col", 1),), 1)
    padded = jnp.pad(rimmed, ((0, 0), (0, 0), (1, 1)))
    right = (
        own_cols * field + link_cols[0] * padded[:, :-2, 1:-1] + link_cols[1] * padded[:, 2:, 1:-1]
    )
    right = right + link_cols[2] * padded[:, 1:-1, :-2] + link_cols[3] * padded[:, 1:-1, 2:]
    predicted = right.reshape(row_count, col_count).at[local_rows, diag_clip].add(diag_values)
    chosen = wells[0]
    col_local = chosen - col_start
    in_col = (col_local >= 0) & (col_local < col_count)
    col_clip = jnp.clip(col_local, 0, col_count - 1)
    order = jnp.argsort(jnp.where(in_col, 0, 1).astype(jnp.int32), stable=True)[:WMAX]
    valid = in_col[order]
    compact = jnp.where(valid[None, :], jnp.take(predicted, col_clip[order], axis=1), 0.0)
    numbers = jnp.where(valid, order, -1).astype(jnp.float32)
    all_cols, all_numbers = rows_first((compact, numbers), "col", (1, 0))
    onehot = (all_numbers[:, None] == jnp.arange(M, dtype=jnp.float32)[None, :]).astype(jnp.float32)
    strip = jnp.dot(all_cols, onehot, precision=lax.Precision.HIGHEST)
    row_local = chosen - row_start
    in_row = (row_local >= 0) & (row_local < row_count)
    row_clip = jnp.clip(row_local, 0, row_count - 1)
    rows_part = jnp.where(in_row[:, None], jnp.take(predicted, row_clip, axis=0), 0.0)
    gram_part = jnp.where(in_row[:, None], jnp.take(strip, row_clip, axis=0), 0.0)
    across, gram = lax.psum((rows_part, gram_part), "row")
    innovation = gram + jnp.diag(noise[0])
    factor = jnp.linalg.cholesky(innovation)
    solved = jax.scipy.linalg.cho_solve((factor, True), across)
    current = predicted - jnp.dot(strip, solved, precision=lax.Precision.HIGHEST)
    return current


def solution(mesh):
    in_specs = (P("row", "col"), P(), P(), P(), P(), P())
    out_specs = P("row", "col")
    return jax.shard_map(shards, mesh=mesh, in_specs=in_specs, out_specs=out_specs, check_vma=False)
```

profile of v0, /device:TPU:0, one launch (start us, length us, event | category | flops | bytes accessed | tf_op | source)
XLA Modules:
  0.0 419.2 jit_solution(4098314979119295900)
XLA Ops:
  6.5 1.3 slice_bitcast_fusion.1
  7.8 3.6 collective-permute-start
  11.4 1.3 collective-permute-start.1
  12.8 0.7 and_reduce_fusion.1
  13.5 0.7 subtract_clamp_fusion.1
  14.1 0.7 dynamic-slice_select_fusion
  14.9 3.2 sort.17
  18.0 0.7 gather_fusion
  18.8 0.7 gather_fusion.1
  19.5 1.0 constant_dynamic-slice_fusion.1
  20.5 2.0 collective-permute-done
  22.6 13.5 %collective-permute-done.1 = f32[1,128,1024]{2,1,0:T(8,128)S(1)} collective-permute-done((f32[1,128,1024]{2,1,0:T(8,128)S(1)}, f32[1,128,1024]{2,1,0:T(8,128)S(1)}, u32[]{:S(2)}, u32[]{:S(2)}) %collective-permute-start.1) | collective-permute-done | bytes 524320 | tf_op jit(solution)/shard_map/ppermute | solution.py:21
  36.1 4.3 %select_maximum_fusion.2 = f32[18,130,1024]{2,1,0:T(8,128)S(1)} fusion(f32[1,128,1024]{2,1,0:T(8,128)S(1)} %collective-permute-done.1, f32[16,128,1024]{2,1,0:T(8,128)} %bitcast.73, f32[1,128,1024]{2,1,0:T(8,128)S(1)} %collective-permute-done), kind=kLoop, calls=%fused_computation.15 | loop fusion | flops 19169280 | bytes 19021824 | tf_op jit(solution)/shard_map/concatenate | solution.py:17
  40.3 9.5 %fusion.9 = f32[16,128,1024]{2,1,0:T(8,128)S(1)} fusion(f32[18,130,1024]{2,1,0:T(8,128)S(1)} %select_maximum_fusion.2, f32[1,128,1024]{2,1,0:T(8,128)S(1)} %collective-permute-done.1, f32[16,128,1024]{2,1,0:T(8,128)} %bitcast.74, f32[1,128,1024]{2,1,0:T(8,128)S(1)} %collective-permute-done, f32[16,128]{1,0:T(8,128)S(1)} %bitcast.79, ...), kind=kLoop, calls=%fused_computation.30 | loop fusion | flops 23068672 | bytes 34643968 | tf_op jit(solution)/shard_map/add | solution.py:69
  49.9 2.1 copy.32
  52.0 3.4 copy-done.2
  55.4 2.1 fusion.38
  57.5 1.3 collective-permute-start.2
  58.8 1.8 collective-permute-start.3
  60.7 0.9 constant_dynamic-slice_fusion.2
  61.8 0.1 and_reduce_fusion
  62.0 4.8 %collective-permute-done.3 = f32[2048,1,128]{2,1,0:T(1,128)S(1)} collective-permute-done((f32[2048,1,128]{2,1,0:T(1,128)S(1)}, f32[2048,1,128]{2,1,0:T(1,128)S(1)}, u32[]{:S(2)}, u32[]{:S(2)}) %collective-permute-start.3) | collective-permute-done | bytes 1048608 | tf_op jit(solution)/shard_map/ppermute | solution.py:21
  66.8 23.3 %select_maximum_fusion = f32[2048,10,130]{2,1,0:T(8,128)} fusion(f32[2048,1,128]{2,1,0:T(1,128)S(1)} %collective-permute-done.3, f32[2048,8,128]{2,1,0:T(8,128)} %bitcast.71, f32[2048,1,128]{2,1,0:T(1,128)S(1)} %collective-permute-done.2), kind=kLoop, calls=%fused_computation.10 | loop fusion | flops 21299200 | bytes 21135360 | tf_op jit(solution)/shard_map/concatenate | solution.py:17
  90.0 32.2 %fusion.3 = f32[2097152]{0:T(1024)} fusion(f32[2048,10,130]{2,1,0:T(8,128)} %select_maximum_fusion, f32[2048,1,128]{2,1,0:T(1,128)S(1)} %collective-permute-done.3, f32[2048,8,128]{2,1,0:T(8,128)} %bitcast.72, f32[2048,1,128]{2,1,0:T(1,128)S(1)} %collective-permute-done.2, f32[8,128]{1,0:T(8,128)S(1)} %bitcast.83, f32[8,128]{1,0:T(8,128)S(1)} %bitcast.81, ...), kind=kLoop, calls=%fused_computation.20 | loop fusion | flops 23068672 | bytes 35672064
  122.3 16.9 %scatter_fusion = f32[2097152]{0:T(1024)} fusion(f32[2097152]{0:T(1024)} %fusion.3, s32[2048]{0:T(1024)S(1)} %broadcast_select_fusion, f32[2048]{0:T(1024)S(1)} %dynamic-slice_select_fusion), kind=kCustom, calls=%fused_computation.5 | custom fusion | flops 2048 | bytes 32768
  139.1 9.2 %reshape.178 = f32[2048,1024]{1,0:T(8,128)} reshape(f32[2097152]{0:T(1024)} %scatter_fusion) | data formatting | bytes 16777216 | tf_op jit(solution)/shard_map/scatter-add | solution.py:77
  148.4 9.1 %copy.23 = f32[2048,1024]{0,1:T(8,128)} copy(f32[2048,1024]{1,0:T(8,128)} %reshape.178) | data formatting | bytes 16777216 | tf_op jit(solution)/shard_map/scatter-add | solution.py:77
  157.5 4.2 gather_fusion.2
  161.7 0.1 select_select_fusion.2
  161.8 0.7 pad_maximum_fusion.4
  162.5 0.2 all-reduce.6.cloned.1.call-start
  162.8 5.0 %gather_fusion.4 = f32[256,1024]{1,0:T(8,128)S(1)} fusion(f32[2048,1024]{1,0:T(8,128)} %reshape.178, s32[1024]{0:T(1024)S(1)} %pad_clamp_fusion), kind=kCustom, calls=%fused_computation.4 | custom fusion | bytes 2098176 | tf_op jit(solution)/shard_map/jit(_take)/gather | solution.py:92
  167.8 1.2 select_select_fusion
  168.9 72.6 %all-gather.2.cloned.1.call-done = f32[512,2049]{1,0:T(8,128)} async-done(((f32[32,2049]{1,0:T(8,128)}), f32[512,2049]{1,0:T(8,128)}) %all-gather.2.cloned.1.call-update) | async-done | bytes 4196368 | tf_op jit(solution)/shard_map/all_gather | solution.py:32
  241.6 1.1 slice_reduce_fusion
  242.7 5.7 %fusion.15 = f32[2048,256]{1,0:T(8,128)S(1)} fusion(f32[512,2049]{1,0:T(8,128)} %all-gather.2.cloned.1.call-done, f32[512]{0:T(512)S(1)} %slice_reduce_fusion), kind=kOutput, calls=%fused_computation.40 | convolution fusion | flops 3221356544 | bytes 6293504 | tf_op jit(solution)/shard_map/dot_general | solution.py:88
  248.4 1.0 gather_fusion.3
  249.3 0.1 copy.25
  249.5 0.7 select_select_fusion.3
  250.3 82.6 %all-reduce.6.cloned.1.call-done = (f32[256,1024]{1,0:T(8,128)}, f32[256,256]{0,1:T(8,128)}) async-done(((f32[256,1024]{1,0:T(8,128)}, f32[256,256]{0,1:T(8,128)}), (f32[256,1024]{1,0:T(8,128)}, f32[256,256]{0,1:T(8,128)})) %all-reduce.6.cloned.1.call-update) | async-done | bytes 1310736 | tf_op jit(solution)/shard_map/psum | solution.py:94
  332.8 1.0 select_add_fusion
  333.8 0.1 copy.26
  333.9 1.0 fusion.22
  334.9 11.7 %cholesky.48 = f32[128,128]{1,0:T(8,128)S(1)} custom-call(f32[128,128]{1,0:T(8,128)S(1)} %cholesky.112), custom_call_target="Cholesky" | custom-call | tf_op jit(solution)/shard_map/jit(cholesky)/cholesky | solution.py:96
  346.7 9.8 %custom-call.18 = f32[1,128,128]{1,2,0:T(8,128)S(1)} custom-call(f32[1,128,128]{2,1,0:T(8,128)S(1)} %get-tuple-element.56), custom_call_target="InvertDiagBlocksLowerTriangular" | custom-call | tf_op jit(solution)/shard_map/jit(cholesky)/cholesky | solution.py:96
  356.5 0.2 fusion.24
  356.7 0.3 convolution_subtract_fusion.3
  357.0 11.9 %cholesky.101 = f32[128,128]{1,0:T(8,128)S(1)} custom-call(f32[128,128]{1,0:T(8,128)S(1)} %convolution_subtract_fusion.3), custom_call_target="Cholesky" | custom-call | tf_op jit(solution)/shard_map/jit(cholesky)/cholesky | solution.py:96
  369.1 0.1 copy.28
  369.2 0.1 copy.27
  369.3 0.7 compare_reduce_fusion
  371.4 4.3 %while.1 = (s32[]{:T(128)}, f32[256,256]{0,1:T(8,128)S(1)}, s32[2,2]{1,0:T(2,128)S(1)}, f32[2,128,128]{2,1,0:T(8,128)S(1)}, s32[]{:T(128)}) while((s32[]{:T(128)}, f32[256,256]{0,1:T(8,128)S(1)}, s32[2,2]{1,0:T(2,128)S(1)}, f32[2,128,128]{2,1,0:T(8,128)S(1)}, s32[]{:T(128)}) %tuple.34), condition=%wide.while_cond, body=%wide.while_body.sunk | while | flops 2 | bytes 393321 | solution.py:97
  371.4 0.7 fusion.48
  372.1 1.3 dynamic-slice.23
  373.6 0.7 fusion.48
  374.2 1.3 dynamic-slice.23
  375.7 19.7 %custom-call.19 = f32[2,128,128]{1,2,0:T(8,128)S(1)} custom-call(f32[2,128,128]{2,1,0:T(8,128)S(1)} %get-tuple-element.14), custom_call_target="InvertDiagBlocksLowerTriangular" | custom-call | tf_op jit(solution)/shard_map/jit(_cho_solve)/triangular_solve | solution.py:97
  395.4 1.7 fusion.20
  397.0 1.7 convolution_subtract_fusion.2
  398.7 0.6 fusion.29
  399.4 0.6 fusion.28
  400.0 0.6 convolution_subtract_fusion.1
  400.6 0.6 fusion.27
  401.1 11.0 %convolution_subtract_fusion = f32[2048,1024]{1,0:T(8,128)} fusion(f32[2048,1024]{1,0:T(8,128)} %reshape.178, f32[2048,256]{1,0:T(8,128)S(1)} %fusion.15, f32[128,1024]{1,0:T(8,128)S(1)} %fusion.28, f32[128,1024]{1,0:T(8,128)S(1)} %fusion.27), kind=kOutput, calls=%fused_computation.39 | convolution fusion | flops 6444810240 | bytes 19922944 | tf_op jit(solution)/shard_map/dot_general | solution.py:98
  (52 shorter events, 0.9 us)
Async XLA Ops:
  6.5 7.6 %copy-start = (f32[16384]{0:T(1024)S(1)}, f32[16384]{0:T(1024)}, u32[]{:S(2)}) copy-start(f32[16384]{0:T(1024)} %param.7) | copy-start | bytes 196612
  6.5 235.0 %all-gather.2.cloned.1.call-start = ((), (), s32[]{:S(2)}) async-start(), calls=%async_computation | async-start | bytes 4734976 | tf_op jit(solution)/shard_map/all_gather | solution.py:32
  7.8 14.7 %collective-permute-start = (f32[1,128,1024]{2,1,0:T(8,128)S(1)}, f32[1,128,1024]{2,1,0:T(8,128)S(1)}, u32[]{:S(2)}, u32[]{:S(2)}) collective-permute-start(f32[1,128,1024]{2,1,0:T(8,128)S(1)} %get-tuple-element.45), channel_id=1, source_target_pairs={{0,16},{16,32},{32,48},{48,64},{64,80},{80,96},{96,112},{1,17},{17... | collective-permute-start | bytes 1572872 | tf_op jit(solution)/shard_map/ppermute | solution.py:19
  11.4 24.6 %collective-permute-start.1 = (f32[1,128,1024]{2,1,0:T(8,128)S(1)}, f32[1,128,1024]{2,1,0:T(8,128)S(1)}, u32[]{:S(2)}, u32[]{:S(2)}) collective-permute-start(f32[1,128,1024]{2,1,0:T(8,128)S(1)} %get-tuple-element.46), channel_id=1, source_target_pairs={{16,0},{32,16},{48,32},{64,48},{80,64},{96,80},{112,96},{17,1},{33... | collective-permute-start | bytes 1572872 | tf_op jit(solution)/shard_map/ppermute | solution.py:21
  49.9 11.8 %copy-start.6 = (s32[2]{0:T(128)S(1)}, s32[2]{0:T(128)}, u32[]{:S(2)}) copy-start(s32[2]{0:T(128)} %constant.169) | copy-start | bytes 28
  49.9 11.9 %copy-start.5 = (s32[2]{0:T(128)S(1)}, s32[2]{0:T(128)}, u32[]{:S(2)}) copy-start(s32[2]{0:T(128)} %constant.172) | copy-start | bytes 28
  52.0 3.4 copy-start.2
  57.5 4.5 %collective-permute-start.2 = (f32[2048,1,128]{2,1,0:T(1,128)}, f32[2048,1,128]{2,1,0:T(1,128)S(1)}, u32[]{:S(2)}, u32[]{:S(2)}) collective-permute-start(f32[2048,1,128]{2,1,0:T(1,128)} %get-tuple-element.43), channel_id=1, source_target_pairs={{0,1},{1,2},{2,3},{3,4},{4,5},{5,6},{6,7},{7,8},{8,9},{9,10},{10,1... | collective-permute-start | bytes 3145736 | tf_op jit(solution)/shard_map/ppermute | solution.py:19
  58.8 7.9 %collective-permute-start.3 = (f32[2048,1,128]{2,1,0:T(1,128)S(1)}, f32[2048,1,128]{2,1,0:T(1,128)S(1)}, u32[]{:S(2)}, u32[]{:S(2)}) collective-permute-start(f32[2048,1,128]{2,1,0:T(1,128)S(1)} %get-tuple-element.44), channel_id=1, source_target_pairs={{1,0},{2,1},{3,2},{4,3},{5,4},{6,5},{7,6},{8,7},{9,8},{10,9},{11,1... | collective-permute-start | bytes 3145736 | tf_op jit(solution)/shard_map/ppermute | solution.py:21
  157.5 5.3 %copy-start.3 = (s32[1,256]{1,0:T(1,128)S(1)}, s32[1,256]{1,0:T(1,128)}, u32[]{:S(2)}) copy-start(s32[1,256]{1,0:T(1,128)} %param.10) | copy-start | bytes 3076
  162.5 170.3 %all-reduce.6.cloned.1.call-start = ((), (), s32[]{:S(2)}) async-start(), calls=%async_computation.1 | async-start | bytes 2621440 | tf_op jit(solution)/shard_map/psum | solution.py:94
  167.8 165.1 %copy-start.4 = (f32[1,256]{1,0:T(1,128)S(1)}, f32[1,256]{1,0:T(1,128)}, u32[]{:S(2)}) copy-start(f32[1,256]{1,0:T(1,128)} %param.11) | copy-start | bytes 3076
  400.5 11.6 %copy-start.1 = (f32[16384]{0:T(1024)S(1)}, f32[16384]{0:T(1024)}, u32[]{:S(2)}) copy-start(f32[16384]{0:T(1024)} %param.7) | copy-start | bytes 196612
Sparse Core Ops, SparseCore 0:
  162.7 78.8 all-gather.1
  250.4 82.4 all-reduce.5
where the time goes:
time: 425 us; the launch traced here: 419 us
  waiting for transfers between devices  176 us (41%)
  other arithmetic  150 us (35%)
  local copies, waits for them, and re-layouts  46.8 us (11%)
  matrix products  22.9 us (5%)
  between operations  15.3 us (4%)
  starting transfers between devices  8.21 us (2%)
    psum x1, waiting for transfers between devices, shards(): across, gram = lax.psum((rows_part, gram_part), 'row')  82.6 us
    all_gather x1, waiting for transfers between devices, rows_first(): result = lax.all_gather(both, axis, axis=0, tiled=True)  72.6 us
    unnamed x6, other arithmetic  49.3 us
    another operation x6, other arithmetic, shards(): factor = jnp.linalg.cholesky(innovation)  34.2 us
    concatenate x2, other arithmetic, extended(): jnp.concatenate([lax.ppermute(tail, axis, [(i, (i + 1) % count) for i in...  27.6 us
    another operation x3, other arithmetic, shards(): solved = jax.scipy.linalg.cho_solve((factor, True), across)  19.7 us
    scatter-add x2, local copies, waits for them, and re-layouts, shards(): right.reshape(row_count, col_count).at[local_rows, diag_clip]  18.4 us
    ppermute x2, waiting for transfers between devices, extended(): lax.ppermute(head, axis, [((i + 1) % count, i) for i in range(ends)])  18.3 us
  transfers between devices with their start and end apart: 6, of which 5 were waited for; matrix products, arithmetic and copies ran while one was open for 4% of the time, Pallas kernels for 0%

commit v1 on v0

--- a/solution.py
+++ b/solution.py
@@ -6,6 +6,11 @@
 NGY = 128
 M = 256
 WMAX = 32
+
+
+def gather_over(value, axis, dim):
+    sent = jnp.stack([value] * lax.axis_size(axis))
+    return jnp.concatenate(lax.all_to_all(sent, axis, 0, 0), axis=dim)
 
 
 def extended(cells, sides, width):
@@ -29,7 +34,7 @@
     turned = [jnp.moveaxis(a, dim, 0) for a, dim in zip(arrays, dims)]
     widths = [t[0].size for t in turned]
     both = jnp.concatenate([t.reshape(-1, w) for t, w in zip(turned, widths)], axis=1)
-    result = lax.all_gather(both, axis, axis=0, tiled=True)
+    result = gather_over(both, axis, 0)
     blocks = jnp.split(result, [sum(widths[:k]) for k in range(1, len(widths))], axis=1)
     return tuple(
         (

time: 425 us -> 441 us (1.038)
  starting transfers between devices: 8.21 us -> 35.1 us
  waiting for transfers between devices: 176 us -> 162 us
    all_gather x1 -> x0, waiting for transfers between devices: 72.6 us -> none  [rows_first(): result = lax.all_gather(both, axis, axis=0, tiled=True)]
    all_to_all x0 -> x1, waiting for transfers between devices: none -> 50 us  [gather_over(): return jnp.concatenate(lax.all_to_all(sent, axis, 0, 0), axis=dim)]
    all_to_all x0 -> x1, starting transfers between devices: none -> 26.9 us  [gather_over(): return jnp.concatenate(lax.all_to_all(sent, axis, 0, 0), axis=dim)]
    psum x1, waiting for transfers between devices: 82.6 us -> 91.9 us  [shards(): across, gram = lax.psum((rows_part, gram_part), 'row')]
where the time goes in v1:
time: 441 us; the launch traced here: 435 us
  waiting for transfers between devices  162 us (37%)
  other arithmetic  150 us (34%)
  local copies, waits for them, and re-layouts  49.3 us (11%)
  starting transfers between devices  35.1 us (8%)
  matrix products  22.9 us (5%)
  between operations  15.4 us (3%)
    psum x1, waiting for transfers between devices, shards(): across, gram = lax.psum((rows_part, gram_part), 'row')  91.9 us
    all_to_all x1, waiting for transfers between devices, gather_over(): return jnp.concatenate(lax.all_to_all(sent, axis, 0, 0), axis=dim)  50 us
    unnamed x6, other arithmetic  49.3 us
    another operation x6, other arithmetic, shards(): factor = jnp.linalg.cholesky(innovation)  34.2 us
    concatenate x2, other arithmetic, extended(): jnp.concatenate([lax.ppermute(tail, axis, [(i, (i + 1) % count) for i in...  27.6 us
    all_to_all x1, starting transfers between devices, gather_over(): return jnp.concatenate(lax.all_to_all(sent, axis, 0, 0), axis=dim)  26.9 us
    another operation x3, other arithmetic, shards(): solved = jax.scipy.linalg.cho_solve((factor, True), across)  19.7 us
    scatter-add x2, local copies, waits for them, and re-layouts, shards(): right.reshape(row_count, col_count).at[local_rows, diag_clip]  18.4 us
  transfers between devices with their start and end apart: 6, of which 5 were waited for; matrix products, arithmetic and copies ran while one was open for 4% of the time, Pallas kernels for 0%

profile of v1, /device:TPU:0, one launch (start us, length us, event | category | flops | bytes accessed | tf_op | source)
XLA Modules:
  0.0 434.6 jit_solution(6711457977138542496)
XLA Ops:
  6.5 1.3 slice_bitcast_fusion.1
  7.8 3.6 collective-permute-start
  11.4 1.3 collective-permute-start.1
  12.8 0.7 and_reduce_fusion.1
  13.5 0.7 subtract_clamp_fusion.1
  14.1 0.7 dynamic-slice_select_fusion
  14.9 3.2 sort.17
  18.0 0.7 gather_fusion
  18.8 0.7 gather_fusion.1
  19.5 1.0 constant_dynamic-slice_fusion.1
  20.5 2.0 collective-permute-done
  22.6 13.5 %collective-permute-done.1 = f32[1,128,1024]{2,1,0:T(8,128)S(1)} collective-permute-done((f32[1,128,1024]{2,1,0:T(8,128)S(1)}, f32[1,128,1024]{2,1,0:T(8,128)S(1)}, u32[]{:S(2)}, u32[]{:S(2)}) %collective-permute-start.1) | collective-permute-done | bytes 524320 | tf_op jit(solution)/shard_map/ppermute | solution.py:26
  36.1 4.3 select_maximum_fusion.2
  40.3 9.5 %fusion.9 = f32[16,128,1024]{2,1,0:T(8,128)S(1)} fusion(f32[18,130,1024]{2,1,0:T(8,128)S(1)} %select_maximum_fusion.2, f32[1,128,1024]{2,1,0:T(8,128)S(1)} %collective-permute-done.1, f32[16,128,1024]{2,1,0:T(8,128)} %bitcast.75, f32[1,128,1024]{2,1,0:T(8,128)S(1)} %collective-permute-done, f32[16,128]{1,0:T(8,128)S(1)} %bitcast.80, ...), kind=kLoop, calls=%fused_computation.30 | loop fusion | flops 23068672 | bytes 34643968 | tf_op jit(solution)/shard_map/add | solution.py:74
  49.9 2.1 copy.41
  52.0 3.4 copy-done.2
  55.4 2.1 fusion.38
  57.5 1.3 collective-permute-start.2
  58.8 1.8 collective-permute-start.3
  60.7 0.9 constant_dynamic-slice_fusion.2
  61.8 0.1 and_reduce_fusion
  62.0 4.8 %collective-permute-done.3 = f32[2048,1,128]{2,1,0:T(1,128)S(1)} collective-permute-done((f32[2048,1,128]{2,1,0:T(1,128)S(1)}, f32[2048,1,128]{2,1,0:T(1,128)S(1)}, u32[]{:S(2)}, u32[]{:S(2)}) %collective-permute-start.3) | collective-permute-done | bytes 1048608 | tf_op jit(solution)/shard_map/ppermute | solution.py:26
  66.8 23.3 %select_maximum_fusion = f32[2048,10,130]{2,1,0:T(8,128)} fusion(f32[2048,1,128]{2,1,0:T(1,128)S(1)} %collective-permute-done.3, f32[2048,8,128]{2,1,0:T(8,128)} %bitcast.72, f32[2048,1,128]{2,1,0:T(1,128)S(1)} %collective-permute-done.2), kind=kLoop, calls=%fused_computation.10 | loop fusion | flops 21299200 | bytes 21135360 | tf_op jit(solution)/shard_map/concatenate | solution.py:22
  90.0 32.2 %fusion.3 = f32[2097152]{0:T(1024)} fusion(f32[2048,10,130]{2,1,0:T(8,128)} %select_maximum_fusion, f32[2048,1,128]{2,1,0:T(1,128)S(1)} %collective-permute-done.3, f32[2048,8,128]{2,1,0:T(8,128)} %bitcast.73, f32[2048,1,128]{2,1,0:T(1,128)S(1)} %collective-permute-done.2, f32[8,128]{1,0:T(8,128)S(1)} %bitcast.84, f32[8,128]{1,0:T(8,128)S(1)} %bitcast.82, ...), kind=kLoop, calls=%fused_computation.20 | loop fusion | flops 23068672 | bytes 35672064
  122.3 16.9 %scatter_fusion = f32[2097152]{0:T(1024)} fusion(f32[2097152]{0:T(1024)} %fusion.3, s32[2048]{0:T(1024)S(1)} %broadcast_select_fusion, f32[2048]{0:T(1024)S(1)} %dynamic-slice_select_fusion), kind=kCustom, calls=%fused_computation.5 | custom fusion | flops 2048 | bytes 32768
  139.1 9.2 %reshape.184 = f32[2048,1024]{1,0:T(8,128)} reshape(f32[2097152]{0:T(1024)} %scatter_fusion) | data formatting | bytes 16777216 | tf_op jit(solution)/shard_map/scatter-add | solution.py:82
  148.4 9.1 %copy.32 = f32[2048,1024]{0,1:T(8,128)} copy(f32[2048,1024]{1,0:T(8,128)} %reshape.184) | data formatting | bytes 16777216 | tf_op jit(solution)/shard_map/scatter-add | solution.py:82
  157.5 4.1 gather_fusion.2
  161.7 0.1 select_select_fusion.2
  161.8 2.5 stack.2
  164.3 26.9 %all-to-all-start = ((f32[16,32,2049]{2,1,0:T(8,128)}), f32[16,32,2049]{2,1,0:T(8,128)}, u32[]{:S(2)}, u32[]{:S(2)}) async-start(f32[16,32,2049]{2,1,0:T(8,128)} %stack.2), calls=%async_computation | async-start | bytes 8912896 | tf_op jit(solution)/shard_map/all_to_all | solution.py:13
  191.2 0.2 all-reduce.6.cloned.1.call-start
  191.5 5.0 %gather_fusion.4 = f32[256,1024]{1,0:T(8,128)S(1)} fusion(f32[2048,1024]{1,0:T(8,128)} %reshape.184, s32[1024]{0:T(1024)S(1)} %pad_clamp_fusion), kind=kCustom, calls=%fused_computation.4 | custom fusion | bytes 2098176 | tf_op jit(solution)/shard_map/jit(_take)/gather | solution.py:97
  196.4 1.2 select_select_fusion
  197.7 50.0 %all-to-all-done = f32[16,32,2049]{2,1,0:T(8,128)} async-done(((f32[16,32,2049]{2,1,0:T(8,128)}), f32[16,32,2049]{2,1,0:T(8,128)}, u32[]{:S(2)}, u32[]{:S(2)}) %all-to-all-start) | async-done | bytes 4196384 | tf_op jit(solution)/shard_map/all_to_all | solution.py:13
  247.7 1.1 slice_reduce_fusion
  248.8 5.7 %fusion.15 = f32[2048,256]{1,0:T(8,128)S(1)} fusion(f32[512,2049]{1,0:T(8,128)} %bitcast.18, f32[512]{0:T(512)S(1)} %slice_reduce_fusion), kind=kOutput, calls=%fused_computation.40 | convolution fusion | flops 3221356544 | bytes 6293504 | tf_op jit(solution)/shard_map/dot_general | solution.py:93
  254.5 1.0 gather_fusion.3
  255.5 0.1 copy.34
  255.6 0.7 select_select_fusion.3
  256.4 91.9 %all-reduce.6.cloned.1.call-done = (f32[256,1024]{1,0:T(8,128)}, f32[256,256]{0,1:T(8,128)}) async-done(((f32[256,1024]{1,0:T(8,128)}, f32[256,256]{0,1:T(8,128)}), (f32[256,1024]{1,0:T(8,128)}, f32[256,256]{0,1:T(8,128)})) %all-reduce.6.cloned.1.call-update) | async-done | bytes 1310736 | tf_op jit(solution)/shard_map/psum | solution.py:99
  348.3 1.0 select_add_fusion
  349.2 0.1 copy.35
  349.4 1.0 fusion.22
  350.4 11.7 %cholesky.48 = f32[128,128]{1,0:T(8,128)S(1)} custom-call(f32[128,128]{1,0:T(8,128)S(1)} %cholesky.112), custom_call_target="Cholesky" | custom-call | tf_op jit(solution)/shard_map/jit(cholesky)/cholesky | solution.py:101
  362.1 9.8 %custom-call.18 = f32[1,128,128]{1,2,0:T(8,128)S(1)} custom-call(f32[1,128,128]{2,1,0:T(8,128)S(1)} %get-tuple-element.60), custom_call_target="InvertDiagBlocksLowerTriangular" | custom-call | tf_op jit(solution)/shard_map/jit(cholesky)/cholesky | solution.py:101
  371.9 0.2 fusion.24
  372.2 0.3 convolution_subtract_fusion.3
  372.4 11.9 %cholesky.101 = f32[128,128]{1,0:T(8,128)S(1)} custom-call(f32[128,128]{1,0:T(8,128)S(1)} %convolution_subtract_fusion.3), custom_call_target="Cholesky" | custom-call | tf_op jit(solution)/shard_map/jit(cholesky)/cholesky | solution.py:101
  384.6 0.1 copy.36
  384.7 0.7 compare_reduce_fusion
  386.8 4.3 while.1
  386.8 0.7 fusion.48
  387.5 1.3 dynamic-slice.23
  389.0 0.7 fusion.48
  389.6 1.3 dynamic-slice.23
  391.1 19.7 %custom-call.19 = f32[2,128,128]{1,2,0:T(8,128)S(1)} custom-call(f32[2,128,128]{2,1,0:T(8,128)S(1)} %get-tuple-element.14), custom_call_target="InvertDiagBlocksLowerTriangular" | custom-call | tf_op jit(solution)/shard_map/jit(_cho_solve)/triangular_solve | solution.py:102
  410.8 1.7 fusion.20
  412.5 1.7 convolution_subtract_fusion.2
  414.1 0.6 fusion.29
  414.8 0.6 fusion.28
  415.4 0.6 convolution_subtract_fusion.1
  416.0 0.6 fusion.27
  416.6 11.0 %convolution_subtract_fusion = f32[2048,1024]{1,0:T(8,128)} fusion(f32[2048,1024]{1,0:T(8,128)} %reshape.184, f32[2048,256]{1,0:T(8,128)S(1)} %fusion.15, f32[128,1024]{1,0:T(8,128)S(1)} %fusion.28, f32[128,1024]{1,0:T(8,128)S(1)} %fusion.27), kind=kOutput, calls=%fused_computation.39 | convolution fusion | flops 6444810240 | bytes 19922944 | tf_op jit(solution)/shard_map/dot_general | solution.py:103
  (52 shorter events, 1.0 us)
Async XLA Ops:
  6.5 7.6 %copy-start = (f32[16384]{0:T(1024)S(1)}, f32[16384]{0:T(1024)}, u32[]{:S(2)}) copy-start(f32[16384]{0:T(1024)} %param.7) | copy-start | bytes 196612
  7.8 14.7 %collective-permute-start = (f32[1,128,1024]{2,1,0:T(8,128)S(1)}, f32[1,128,1024]{2,1,0:T(8,128)S(1)}, u32[]{:S(2)}, u32[]{:S(2)}) collective-permute-start(f32[1,128,1024]{2,1,0:T(8,128)S(1)} %get-tuple-element.49), channel_id=1, source_target_pairs={{0,16},{16,32},{32,48},{48,64},{64,80},{80,96},{96,112},{1,17},{17... | collective-permute-start | bytes 1572872 | tf_op jit(solution)/shard_map/ppermute | solution.py:24
  11.4 24.6 %collective-permute-start.1 = (f32[1,128,1024]{2,1,0:T(8,128)S(1)}, f32[1,128,1024]{2,1,0:T(8,128)S(1)}, u32[]{:S(2)}, u32[]{:S(2)}) collective-permute-start(f32[1,128,1024]{2,1,0:T(8,128)S(1)} %get-tuple-element.50), channel_id=1, source_target_pairs={{16,0},{32,16},{48,32},{64,48},{80,64},{96,80},{112,96},{17,1},{33... | collective-permute-start | bytes 1572872 | tf_op jit(solution)/shard_map/ppermute | solution.py:26
  49.9 11.8 %copy-start.6 = (s32[2]{0:T(128)S(1)}, s32[2]{0:T(128)}, u32[]{:S(2)}) copy-start(s32[2]{0:T(128)} %constant.169) | copy-start | bytes 28
  49.9 11.9 %copy-start.5 = (s32[2]{0:T(128)S(1)}, s32[2]{0:T(128)}, u32[]{:S(2)}) copy-start(s32[2]{0:T(128)} %constant.172) | copy-start | bytes 28
  52.0 3.4 copy-start.2
  57.5 4.5 %collective-permute-start.2 = (f32[2048,1,128]{2,1,0:T(1,128)}, f32[2048,1,128]{2,1,0:T(1,128)S(1)}, u32[]{:S(2)}, u32[]{:S(2)}) collective-permute-start(f32[2048,1,128]{2,1,0:T(1,128)} %get-tuple-element.47), channel_id=1, source_target_pairs={{0,1},{1,2},{2,3},{3,4},{4,5},{5,6},{6,7},{7,8},{8,9},{9,10},{10,1... | collective-permute-start | bytes 3145736 | tf_op jit(solution)/shard_map/ppermute | solution.py:24
  58.8 7.9 %collective-permute-start.3 = (f32[2048,1,128]{2,1,0:T(1,128)S(1)}, f32[2048,1,128]{2,1,0:T(1,128)S(1)}, u32[]{:S(2)}, u32[]{:S(2)}) collective-permute-start(f32[2048,1,128]{2,1,0:T(1,128)S(1)} %get-tuple-element.48), channel_id=1, source_target_pairs={{1,0},{2,1},{3,2},{4,3},{5,4},{6,5},{7,6},{8,7},{9,8},{10,9},{11,1... | collective-permute-start | bytes 3145736 | tf_op jit(solution)/shard_map/ppermute | solution.py:26
  161.6 29.8 %copy-start.3 = (s32[1,256]{1,0:T(1,128)S(1)}, s32[1,256]{1,0:T(1,128)}, u32[]{:S(2)}) copy-start(s32[1,256]{1,0:T(1,128)} %param.10) | copy-start | bytes 3076
  164.3 83.4 %all-to-all-start = ((f32[16,32,2049]{2,1,0:T(8,128)}), f32[16,32,2049]{2,1,0:T(8,128)}, u32[]{:S(2)}, u32[]{:S(2)}) async-start(f32[16,32,2049]{2,1,0:T(8,128)} %stack.2), calls=%async_computation | async-start | bytes 8912896 | tf_op jit(solution)/shard_map/all_to_all | solution.py:13
  191.2 157.1 %all-reduce.6.cloned.1.call-start = ((), (), s32[]{:S(2)}) async-start(), calls=%async_computation.1 | async-start | bytes 2621440 | tf_op jit(solution)/shard_map/psum | solution.py:99
  196.4 151.8 %copy-start.4 = (f32[1,256]{1,0:T(1,128)S(1)}, f32[1,256]{1,0:T(1,128)}, u32[]{:S(2)}) copy-start(f32[1,256]{1,0:T(1,128)} %param.11) | copy-start | bytes 3076
  416.0 11.6 %copy-start.1 = (f32[16384]{0:T(1024)S(1)}, f32[16384]{0:T(1024)}, u32[]{:S(2)}) copy-start(f32[16384]{0:T(1024)} %param.7) | copy-start | bytes 196612
Sparse Core Ops, SparseCore 0:
  256.5 91.7 all-reduce.5
